TPU v7x, 128 devices: a whole 4x4x4 slice. The times are simulated.
128 devices in a mesh: group: 8 (over y, core), within: 16 (over z, x).
Axes of the slice: x: 4, y: 4, z: 4, core: 2. Of those that a mesh axis runs over, the one named last changes fastest.
Arguments:
- tokens: bfloat16 [16384, 2048], P(('group', 'within')), may hold values from -6 to 6
- languages: int32 [16384], P(('group', 'within')), may hold values from 0 to 99, as said below
- lang_group: int32 [100], replicated, may hold values from 0 to 7, as said below
- group_gain: float32 [8, 2048], replicated, may hold values from 0.25 to 1.75
- group_w1: bfloat16 [8, 2048, 8192], P('group', None, 'within'), may hold values from -0.125 to 0.125
- group_b1: float32 [8, 8192], P('group', 'within'), may hold values from -3 to 3
- group_w2: bfloat16 [8, 8192, 2048], P('group', 'within'), may hold values from -0.0625 to 0.0625
- group_b2: float32 [8, 2048], replicated, may hold values from -3 to 3
- shared_gain: float32 [2048], replicated, may hold values from 0.25 to 1.75
- shared_w1: bfloat16 [2048, 8192], P(None, 'group'), may hold values from -0.125 to 0.125
- shared_b1: float32 [8192], P('group'), may hold values from -3 to 3
- shared_w2: bfloat16 [8192, 2048], P('group'), may hold values from -0.0625 to 0.0625
- shared_b2: float32 [2048], replicated, may hold values from -3 to 3
Outputs:
- encoded: bfloat16 [16384, 2048], P(('group', 'within'))
Inputs may be any that keep to these rules, and one draw needn't show every extreme that they name: `lang_group`: every language lies in one group and every group holds at least one language. Among the 128 tokens of one device (an aligned block), at most 24 have languages of one group, and in every block some group has exactly 24.
All inputs are finite; a program needn't handle non-finite values.
Results may differ from a plain program's by a relative error of at most 0.017.
Values may be sent and summed in bfloat16 or wider, within the bound.
No kernel may reach another device: no remote copies, remote signals or barrier semaphores. Data moves between devices by JAX's collectives and lax.ppermute only.
A program may use at most 128 MiB of HBM per device.

v0:
```python
import jax
import jax.numpy as jnp
from jax import lax
from jax.sharding import PartitionSpec as P


def layer_norm(values, gains):
    centre = jnp.mean(values, axis=-1, keepdims=True)
    centred = values - centre
    spread = jnp.mean(centred * centred, axis=-1, keepdims=True)
    return centred * lax.rsqrt(spread + 1e-05) * gains


def on_device(
    tokens,
    languages,
    lang_group,
    group_gain,
    group_w1,
    group_b1,
    group_w2,
    group_b2,
    shared_gain,
    shared_w1,
    shared_b1,
    shared_w2,
    shared_b2,
):
    tok_dev = tokens.shape[0]
    width_model = tokens.shape[1]
    num_groups = group_gain.shape[0]
    num_langs = lang_group.shape[0]
    capacity = 3 * tok_dev // (2 * lax.axis_size("group"))
    residual_in = tokens.astype(jnp.float32)
    lang_hit = (languages[:, None] == jnp.arange(num_langs, dtype=jnp.int32)[None, :]).astype(
        jnp.int32
    )
    group_of = jnp.sum(lang_hit * lang_group[None, :], axis=1)
    onehot = (group_of[:, None] == jnp.arange(num_groups, dtype=jnp.int32)[None, :]).astype(
        jnp.int32
    )
    earlier = jnp.cumsum(onehot, axis=0) - onehot
    slot_index = jnp.sum(earlier * onehot, axis=1)
    position = group_of * capacity + slot_index
    dispatch_map = (
        position[None, :] == jnp.arange(num_groups * capacity, dtype=jnp.int32)[:, None]
    ).astype(jnp.bfloat16)
    onehot_float = onehot.astype(jnp.float32)
    row_gains = jnp.dot(onehot_float, group_gain, precision=lax.Precision.HIGHEST)
    normed = layer_norm(residual_in, row_gains).astype(jnp.bfloat16)
    outgoing = jnp.dot(dispatch_map, normed, preferred_element_type=jnp.float32).astype(
        jnp.bfloat16
    )
    outgoing = outgoing.reshape(num_groups, capacity, width_model)
    arrived = lax.all_to_all(outgoing, "group", split_axis=0, concat_axis=0, tiled=True)
    group_rows = arrived.reshape(num_groups * capacity, width_model)
    first_proj = group_w1[0]
    first_bias = group_b1[0]
    second_proj = group_w2[0]
    hidden = jax.nn.relu(
        jnp.dot(
            lax.all_gather(group_rows, "within", axis=0, tiled=True),
            first_proj,
            preferred_element_type=jnp.float32,
        )
        + first_bias
    ).astype(jnp.bfloat16)
    selected = hidden
    summed = lax.psum_scatter(
        jnp.dot(selected, second_proj, preferred_element_type=jnp.float32).astype(jnp.bfloat16),
        "within",
        scatter_dimension=0,
        tiled=True,
    )
    returned = lax.all_to_all(
        summed.reshape(num_groups, capacity, width_model),
        "group",
        split_axis=0,
        concat_axis=0,
        tiled=True,
    )
    returned = returned.reshape(num_groups * capacity, width_model)
    group_out = lax.dot_general(
        dispatch_map, returned, (((0,), (0,)), ((), ())), preferred_element_type=jnp.float32
    )
    group_bias = jnp.dot(onehot_float, group_b2, precision=lax.Precision.HIGHEST)
    middle = residual_in + group_out + group_bias
    shared_in = layer_norm(middle, shared_gain).astype(jnp.bfloat16)
    shared_hidden = jax.nn.relu(
        jnp.dot(
            lax.all_gather(shared_in, "group", axis=0, tiled=True),
            shared_w1,
            preferred_element_type=jnp.float32,
        )
        + shared_b1
    ).astype(jnp.bfloat16)
    selected = shared_hidden
    shared_out = lax.psum_scatter(
        jnp.dot(selected, shared_w2, preferred_element_type=jnp.float32).astype(jnp.bfloat16),
        "group",
        scatter_dimension=0,
        tiled=True,
    ).astype(jnp.float32)
    return (middle + shared_out + shared_b2).astype(jnp.bfloat16)


def solution(mesh):
    placed = (
        P(("group", "within"), None),
        P(("group", "within")),
        P(),
        P(),
        P("group", None, "within"),
        P("group", "within"),
        P("group", "within", None),
        P(),
        P(),
        P(None, "group"),
        P("group"),
        P("group", None),
        P(),
    )
    return jax.shard_map(
        on_device,
        mesh=mesh,
        in_specs=placed,
        out_specs=P(("group", "within"), None),
        check_vma=False,
    )
```

profile of v0, /device:TPU:0, one launch (start us, length us, event | category | flops | bytes accessed | tf_op | source)
XLA Modules:
  0.0 346.0 jit_solution(16796450870467543149)
XLA Ops:
  6.5 0.0 copy-start
  6.5 0.0 all-gather.3.cloned.1.call-start
  6.5 1.3 convert_reduce_fusion
  7.9 1.3 fusion.10
  9.2 0.8 select_reduce_fusion
  10.0 0.1 fusion.17
  10.1 0.2 reduce_window_sum.11
  10.3 0.2 fusion.16
  10.5 2.2 fusion
  12.6 0.4 convolution_convert_fusion.2
  13.0 17.7 %all_to_all.10 = bf16[8,24,2048]{2,1,0:T(8,128)(2,1)} all-to-all(bf16[8,24,2048]{2,1,0:T(8,128)(2,1)S(1)} %bitcast.22), channel_id=1, replica_groups=mesh['group'=8,'within'=16] {'group'}, dimensions={0} | all-to-all | bytes 1572864 | tf_op jit(solution)/shard_map/all_to_all | solution.py:55
  30.7 0.0 all-gather.3.cloned.1.call-update
  30.7 0.0 reduce-scatter.3.cloned.1.call-start
  30.8 90.6 %all-gather.3.cloned.1.call-done = bf16[3072,2048]{1,0:T(8,128)(2,1)} async-done(((bf16[192,2048]{1,0:T(8,128)(2,1)}), bf16[3072,2048]{1,0:T(8,128)(2,1)}) %all-gather.3.cloned.1.call-update) | async-done | bytes 12582928 | tf_op jit(solution)/shard_map/all_gather | solution.py:62
  121.4 0.0 copy-done.6
  121.4 19.5 %convolution_convert_fusion = bf16[3072,2048]{1,0:T(8,128)(2,1)} fusion(bf16[1,512,2048]{2,1,0:T(8,128)(2,1)S(1)} %copy-done, bf16[3072,2048]{1,0:T(8,128)(2,1)} %all-gather.3.cloned.1.call-done, f32[512]{0:T(512)S(1)} %bitcast.24, bf16[1,2048,512]{2,1,0:T(8,128)(2,1)} %param.17), kind=kOutput, calls=%fused_computation | convolution fusion | flops 12895911936 | bytes 29362176 | tf_op jit(solution)/shard_map/dot_general | solution.py:70
  140.8 0.0 reduce-scatter.3.cloned.1.call-update
  140.9 0.0 copy-start.3
  140.9 0.0 all-gather.5.cloned.1.call-start
  140.9 94.3 %reduce-scatter.3.cloned.1.call-done = bf16[192,2048]{1,0:T(8,128)(2,1)} async-done(((bf16[3072,2048]{1,0:T(8,128)(2,1)}), bf16[192,2048]{1,0:T(8,128)(2,1)}) %reduce-scatter.3.cloned.1.call-update) | async-done | bytes 786448 | tf_op jit(solution)/shard_map/reduce_scatter | solution.py:69
  235.2 17.5 %all_to_all.11 = bf16[8,24,2048]{2,1,0:T(8,128)(2,1)S(1)} all-to-all(bf16[8,24,2048]{2,1,0:T(8,128)(2,1)} %bitcast.23), channel_id=1, replica_groups=mesh['group'=8,'within'=16] {'group'}, dimensions={0} | all-to-all | bytes 1572864 | tf_op jit(solution)/shard_map/all_to_all | solution.py:75
  252.7 0.4 convolution_add_fusion.1
  253.1 1.1 fusion.24
  254.3 0.3 multiply_reduce_fusion
  254.5 1.0 multiply_convert_fusion
  255.5 0.0 all-gather.5.cloned.1.call-update
  255.6 0.2 reduce-scatter.5.cloned.1.call-start
  255.8 29.2 %all-gather.5.cloned.1.call-done = bf16[1024,2048]{1,0:T(8,128)(2,1)} async-done(((bf16[128,2048]{1,0:T(8,128)(2,1)}), bf16[1024,2048]{1,0:T(8,128)(2,1)}) %all-gather.5.cloned.1.call-update) | async-done | bytes 4194320 | tf_op jit(solution)/shard_map/all_gather | solution.py:91
  285.0 14.3 %convolution_convert_fusion.1 = bf16[1024,2048]{1,0:T(8,128)(2,1)} fusion(bf16[1024,2048]{1,0:T(8,128)(2,1)} %param.24, f32[1024]{0:T(1024)S(1)} %copy-done.5, bf16[1024,2048]{1,0:T(8,128)(2,1)} %all-gather.5.cloned.1.call-done, bf16[2048,1024]{1,0:T(8,128)(2,1)} %param.22), kind=kOutput, calls=%fused_computation.3 | convolution fusion | flops 8595177472 | bytes 16781312 | tf_op jit(solution)/shard_map/dot_general | solution.py:99
  299.3 0.0 reduce-scatter.5.cloned.1.call-update
  299.4 38.1 %reduce-scatter.5.cloned.1.call-done = bf16[128,2048]{1,0:T(8,128)(2,1)} async-done(((bf16[1024,2048]{1,0:T(8,128)(2,1)}), bf16[128,2048]{1,0:T(8,128)(2,1)}) %reduce-scatter.5.cloned.1.call-update) | async-done | bytes 524304 | tf_op jit(solution)/shard_map/reduce_scatter | solution.py:98
  337.5 2.0 add_convert_fusion
  (16 shorter events, 0.1 us)
Async XLA Ops:
  6.5 114.8 %copy-start = (bf16[1,512,2048]{2,1,0:T(8,128)(2,1)S(1)}, bf16[1,512,2048]{2,1,0:T(8,128)(2,1)}, u32[]{:S(2)}) copy-start(bf16[1,512,2048]{2,1,0:T(8,128)(2,1)} %param.19) | copy-start | bytes 6291460
  6.5 114.8 %copy-start.6 = (f32[1,512]{1,0:T(1,128)S(1)}, f32[1,512]{1,0:T(1,128)}, u32[]{:S(2)}) copy-start(f32[1,512]{1,0:T(1,128)} %param.18) | copy-start | bytes 6148
  6.5 114.8 %all-gather.3.cloned.1.call-start = ((), (), s32[]{:S(2)}) async-start(), calls=%async_computation.4 | async-start | bytes 13369344 | tf_op jit(solution)/shard_map/all_gather | solution.py:62
  30.7 204.5 %reduce-scatter.3.cloned.1.call-start = ((), (), s32[]{:S(2)}) async-start(), calls=%async_computation.5 | async-start | bytes 13369344 | tf_op jit(solution)/shard_map/reduce_scatter | solution.py:69
  140.8 111.9 %copy-start.1 = (bf16[128,2048]{1,0:T(8,128)(2,1)S(1)}, bf16[128,2048]{1,0:T(8,128)(2,1)}, u32[]{:S(2)}) copy-start(bf16[128,2048]{1,0:T(8,128)(2,1)} %param.13) | copy-start | bytes 1572868
  140.8 112.3 %copy-start.2 = (f32[8,2048]{1,0:T(8,128)S(1)}, f32[8,2048]{1,0:T(8,128)}, u32[]{:S(2)}) copy-start(f32[8,2048]{1,0:T(8,128)} %param.20) | copy-start | bytes 196612
  140.9 113.7 %copy-start.3 = (f32[2048]{0:T(1024)S(1)}, f32[2048]{0:T(1024)}, u32[]{:S(2)}) copy-start(f32[2048]{0:T(1024)} %param.21) | copy-start | bytes 24580
  140.9 144.1 %all-gather.5.cloned.1.call-start = ((), (), s32[]{:S(2)}) async-start(), calls=%async_computation.6 | async-start | bytes 4718592 | tf_op jit(solution)/shard_map/all_gather | solution.py:91
  252.7 32.3 %copy-start.5 = (f32[1024]{0:T(1024)S(1)}, f32[1024]{0:T(1024)}, u32[]{:S(2)}) copy-start(f32[1024]{0:T(1024)} %param.23) | copy-start | bytes 12292
  255.6 81.9 %reduce-scatter.5.cloned.1.call-start = ((), (), s32[]{:S(2)}) async-start(), calls=%async_computation.7 | async-start | bytes 4718592 | tf_op jit(solution)/shard_map/reduce_scatter | solution.py:98
  299.3 38.1 %copy-start.4 = (f32[2048]{0:T(1024)S(1)}, f32[2048]{0:T(1024)}, u32[]{:S(2)}) copy-start(f32[2048]{0:T(1024)} %param.25) | copy-start | bytes 24580
Sparse Core Ops, SparseCore 0:
  30.8 90.4 all-gather.2
  141.0 94.1 reduce-scatter.2
  255.7 29.2 all-gather.4
  299.5 37.9 reduce-scatter.4
where the time goes:
time: 346 us
  waiting for transfers between devices  252 us (73%)
  matrix products  37.8 us (11%)
  blocking collectives  35.2 us (10%)
  between operations  13.2 us (4%)
  other arithmetic  7.17 us (2%)
    reduce_scatter x1, waiting for transfers between devices, on_device(): lax.psum_scatter(jnp.dot(selected, second_proj, preferred_element_type=jn...  94.3 us
    all_gather x1, waiting for transfers between devices, on_device(): lax.all_gather(group_rows, 'within', axis=0, tiled=True)  90.6 us
    reduce_scatter x1, waiting for transfers between devices, on_device(): lax.psum_scatter(jnp.dot(selected, shared_w2, preferred_element_type=jnp....  38.1 us
    all_gather x1, waiting for transfers between devices, on_device(): lax.all_gather(shared_in, 'group', axis=0, tiled=True)  29.2 us
    dot_general x1, matrix products, on_device(): jnp.dot(selected, second_proj, preferred_element_type=jnp.float32)  19.5 us
    all_to_all x1, blocking collectives, on_device(): lax.all_to_all(outgoing, 'group', split_axis=0, concat_axis=0, tiled=True)  17.7 us
    all_to_all x1, blocking collectives, on_device(): lax.all_to_all(summed.reshape(num_groups, capacity, width_model), 'group'...  17.5 us
    dot_general x1, matrix products, on_device(): jnp.dot(selected, shared_w2, preferred_element_type=jnp.float32)  14.3 us
  transfers between devices with their start and end apart: 4, of which 4 were waited for; matrix products, arithmetic and copies ran while one was open for 0% of the time, Pallas kernels for 0%

commit v1 on v0

--- a/solution.py
+++ b/solution.py
@@ -26,6 +26,35 @@
     shared_w2,
     shared_b2,
 ):
+
+    def map_task_now(tile_in, dimension_no):
+        axis_name = "group"
+        all_rows = lax.axis_size(axis_name)
+        plain = lax.axis_index(axis_name)
+        s_next, y, reached = (all_rows, plain, tile_in.shape[dimension_no])
+        frames = tuple(((j0, (j0 + 1) % s_next) for j0 in range(s_next)))
+        pool = tuple(((j0, (j0 - 1) % s_next) for j0 in range(s_next)))
+        frame_out = jnp.zeros(
+            (*tile_in.shape[:dimension_no], s_next * reached, *tile_in.shape[dimension_no + 1 :]),
+            tile_in.dtype,
+        )
+        frame_out = lax.dynamic_update_slice_in_dim(
+            frame_out, tile_in, y * reached, axis=dimension_no
+        )
+        inter = prior = tile_in
+        arr_out = s_next // 2
+        for k in tuple(range(1, arr_out + 1)):
+            inter = lax.ppermute(inter, axis_name, perm=frames)
+            frame_out = lax.dynamic_update_slice_in_dim(
+                frame_out, inter, (y - k) % s_next * reached, axis=dimension_no
+            )
+            if k < s_next - arr_out:
+                prior = lax.ppermute(prior, axis_name, pool)
+                frame_out = lax.dynamic_update_slice_in_dim(
+                    frame_out, prior, (y + k) % s_next * reached, axis=dimension_no
+                )
+        return frame_out
+
     tok_dev = tokens.shape[0]
     width_model = tokens.shape[1]
     num_groups = group_gain.shape[0]
@@ -88,9 +117,7 @@
     shared_in = layer_norm(middle, shared_gain).astype(jnp.bfloat16)
     shared_hidden = jax.nn.relu(
         jnp.dot(
-            lax.all_gather(shared_in, "group", axis=0, tiled=True),
-            shared_w1,
-            preferred_element_type=jnp.float32,
+            map_task_now(shared_in, dimension_no=0), shared_w1, preferred_element_type=jnp.float32
         )
         + shared_b1
     ).astype(jnp.bfloat16)

time: 346 us -> 357 us (1.032)
  blocking collectives: 35.2 us -> 17.7 us
  starting transfers between devices: 0.31 us -> 13.4 us
  local copies, waits for them, and re-layouts: 0.03 us -> 12.6 us
    all_gather x1 -> x0, waiting for transfers between devices: 29.2 us -> none  [on_device(): lax.all_gather(shared_in, 'group', axis=0, tiled=True)]
    ppermute x0 -> x7, waiting for transfers between devices: none -> 21.8 us  [the longest x4 20.9 us: map_task_now(): inter = lax.ppermute(inter, axis_name, perm=frames)]
    all_to_all x1 -> x0, blocking collectives: 17.5 us -> none  [on_device(): lax.all_to_all(summed.reshape(num_groups, capacity, width_model), 'group'...]
    all_to_all x0 -> x1, waiting for transfers between devices: none -> 12.9 us  [on_device(): lax.all_to_all(summed.reshape(num_groups, capacity, width_model), 'group'...]
    dynamic_update_slice x0 -> x7, local copies, waits for them, and re-layouts: none -> 10.1 us  [the longest x4 5.47 us: map_task_now(): lax.dynamic_update_slice_in_dim(frame_out, inter, (y - k) % s_next * reac...]
    ppermute x0 -> x7, starting transfers between devices: none -> 8.81 us  [the longest x3 8.8 us: map_task_now(): prior = lax.ppermute(prior, axis_name, pool)]
    all_to_all x0 -> x1, starting transfers between devices: none -> 4.29 us  [on_device(): lax.all_to_all(summed.reshape(num_groups, capacity, width_model), 'group'...]
  transfers between devices with their start and end apart: 4 -> 11, of which waited for: 4 -> 9; matrix products, arithmetic and copies ran while one was open for 0% -> 3% of each run, Pallas kernels for 0% -> 0%
where the time goes in v1:
time: 357 us; the launch traced here: 356 us
  waiting for transfers between devices  255 us (71%)
  matrix products  37.8 us (11%)
  blocking collectives  17.7 us (5%)
  starting transfers between devices  13.4 us (4%)
  between operations  13.2 us (4%)
  local copies, waits for them, and re-layouts  12.6 us (4%)
  other arithmetic  7.15 us (2%)
    reduce_scatter x1, waiting for transfers between devices, on_device(): lax.psum_scatter(jnp.dot(selected, second_proj, preferred_element_type=jn...  94.4 us
    all_gather x1, waiting for transfers between devices, on_device(): lax.all_gather(group_rows, 'within', axis=0, tiled=True)  90.6 us
    reduce_scatter x1, waiting for transfers between devices, on_device(): lax.psum_scatter(jnp.dot(selected, shared_w2, preferred_element_type=jnp....  34.7 us
    ppermute x4, waiting for transfers between devices, map_task_now(): inter = lax.ppermute(inter, axis_name, perm=frames)  20.9 us
    dot_general x1, matrix products, on_device(): jnp.dot(selected, second_proj, preferred_element_type=jnp.float32)  19.4 us
    all_to_all x1, blocking collectives, on_device(): lax.all_to_all(outgoing, 'group', split_axis=0, concat_axis=0, tiled=True)  17.7 us
    dot_general x1, matrix products, on_device(): jnp.dot(selected, shared_w2, preferred_element_type=jnp.float32)  14.4 us
    all_to_all x1, waiting for transfers between devices, on_device(): lax.all_to_all(summed.reshape(num_groups, capacity, width_model), 'group'...  12.9 us
  transfers between devices with their start and end apart: 11, of which 9 were waited for; matrix products, arithmetic and copies ran while one was open for 3% of the time, Pallas kernels for 0%

profile of v1, /device:TPU:0, one launch (start us, length us, event | category | flops | bytes accessed | tf_op | source)
XLA Modules:
  0.0 356.4 jit_solution(5221112802749200692)
XLA Ops:
  6.5 1.3 convert_reduce_fusion
  7.9 1.3 fusion.10
  9.2 0.8 select_reduce_fusion
  10.5 2.2 fusion
  12.6 0.4 convolution_convert_fusion.2
  13.0 17.7 %all_to_all.10 = bf16[8,24,2048]{2,1,0:T(8,128)(2,1)} all-to-all(bf16[8,24,2048]{2,1,0:T(8,128)(2,1)S(1)} %bitcast.22), channel_id=1, replica_groups=mesh['group'=8,'within'=16] {'group'}, dimensions={0} | all-to-all | bytes 1572864 | tf_op jit(solution)/shard_map/all_to_all | solution.py:84
  30.8 90.6 %all-gather.2.cloned.1.call-done = bf16[3072,2048]{1,0:T(8,128)(2,1)} async-done(((bf16[192,2048]{1,0:T(8,128)(2,1)}), bf16[3072,2048]{1,0:T(8,128)(2,1)}) %all-gather.2.cloned.1.call-update) | async-done | bytes 12582928 | tf_op jit(solution)/shard_map/all_gather | solution.py:91
  121.4 19.4 %convolution_convert_fusion = bf16[3072,2048]{1,0:T(8,128)(2,1)} fusion(bf16[1,512,2048]{2,1,0:T(8,128)(2,1)S(1)} %copy-done, bf16[3072,2048]{1,0:T(8,128)(2,1)} %all-gather.2.cloned.1.call-done, f32[512]{0:T(512)S(1)} %bitcast.24, bf16[1,2048,512]{2,1,0:T(8,128)(2,1)} %param.17), kind=kOutput, calls=%fused_computation | convolution fusion | flops 12895911936 | bytes 29362176 | tf_op jit(solution)/shard_map/dot_general | solution.py:99
  140.9 94.4 %reduce-scatter.3.cloned.1.call-done = bf16[192,2048]{1,0:T(8,128)(2,1)} async-done(((bf16[3072,2048]{1,0:T(8,128)(2,1)}), bf16[192,2048]{1,0:T(8,128)(2,1)}) %reduce-scatter.3.cloned.1.call-update) | async-done | bytes 786448 | tf_op jit(solution)/shard_map/reduce_scatter | solution.py:98
  235.3 4.3 %all-to-all-start.1 = ((bf16[8,24,2048]{2,1,0:T(8,128)(2,1)}), bf16[8,24,2048]{2,1,0:T(8,128)(2,1)S(1)}, u32[]{:S(2)}, u32[]{:S(2)}) async-start(bf16[8,24,2048]{2,1,0:T(8,128)(2,1)} %bitcast.23), calls=%async_computation.2 | async-start | bytes 1572864 | tf_op jit(solution)/shard_map/all_to_all | solution.py:104
  239.8 12.9 %all-to-all-done.1 = bf16[8,24,2048]{2,1,0:T(8,128)(2,1)S(1)} async-done(((bf16[8,24,2048]{2,1,0:T(8,128)(2,1)}), bf16[8,24,2048]{2,1,0:T(8,128)(2,1)S(1)}, u32[]{:S(2)}, u32[]{:S(2)}) %all-to-all-start.1) | async-done | bytes 786464 | tf_op jit(solution)/shard_map/all_to_all | solution.py:104
  253.1 1.1 fusion.24
  254.6 2.5 broadcast_in_dim.2
  257.1 1.0 constant_dynamic-update-slice_fusion.6
  258.1 3.0 collective-permute-start.1
  261.0 7.0 %collective-permute-done = bf16[128,2048]{1,0:T(8,128)(2,1)} collective-permute-done((bf16[128,2048]{1,0:T(8,128)(2,1)S(1)}, bf16[128,2048]{1,0:T(8,128)(2,1)}, u32[]{:S(2)}, u32[]{:S(2)}) %collective-permute-start) | collective-permute-done | bytes 524320 | tf_op jit(solution)/shard_map/ppermute | solution.py:47
  268.0 3.0 collective-permute-start.3
  271.0 7.2 %collective-permute-done.2 = bf16[128,2048]{1,0:T(8,128)(2,1)} collective-permute-done((bf16[128,2048]{1,0:T(8,128)(2,1)}, bf16[128,2048]{1,0:T(8,128)(2,1)}, u32[]{:S(2)}, u32[]{:S(2)}) %collective-permute-start.2) | collective-permute-done | bytes 524320 | tf_op jit(solution)/shard_map/ppermute | solution.py:47
  278.1 1.9 constant_dynamic-update-slice_fusion.5
  280.0 1.9 constant_dynamic-update-slice_fusion.4
  281.9 2.9 collective-permute-start.5
  284.8 1.9 constant_dynamic-update-slice_fusion.3
  286.7 1.4 collective-permute-done.4
  288.2 1.9 constant_dynamic-update-slice_fusion.2
  290.0 0.9 constant_dynamic-update-slice_fusion.1
  290.9 0.9 collective-permute-done.5
  291.9 0.8 constant_dynamic-update-slice_fusion
  292.7 5.3 %collective-permute-done.6 = bf16[128,2048]{1,0:T(8,128)(2,1)S(1)} collective-permute-done((bf16[128,2048]{1,0:T(8,128)(2,1)S(1)}, bf16[128,2048]{1,0:T(8,128)(2,1)S(1)}, u32[]{:S(2)}, u32[]{:S(2)}) %collective-permute-start.6) | collective-permute-done | bytes 524320 | tf_op jit(solution)/shard_map/ppermute | solution.py:47
  298.0 0.8 constant_dynamic-update-slice_fusion.7
  298.8 14.4 %convolution_convert_fusion.1 = bf16[1024,2048]{1,0:T(8,128)(2,1)} fusion(bf16[1024,2048]{1,0:T(8,128)(2,1)} %param.24, f32[1024]{0:T(1024)S(1)} %copy-done.5, bf16[1024,2048]{1,0:T(8,128)(2,1)} %constant_dynamic-update-slice_fusion.7, bf16[2048,1024]{1,0:T(8,128)(2,1)} %param.22), kind=kOutput, calls=%fused_computation.3 | convolution fusion | flops 8595177472 | bytes 16781312 | tf_op jit(solution)/shard_map/dot_general | solution.py:126
  313.2 34.7 %reduce-scatter.5.cloned.1.call-done = bf16[128,2048]{1,0:T(8,128)(2,1)} async-done(((bf16[1024,2048]{1,0:T(8,128)(2,1)}), bf16[128,2048]{1,0:T(8,128)(2,1)}) %reduce-scatter.5.cloned.1.call-update) | async-done | bytes 524304 | tf_op jit(solution)/shard_map/reduce_scatter | solution.py:125
  347.9 2.0 add_convert_fusion
  (36 shorter events, 1.4 us)
Async XLA Ops:
  6.5 114.8 %copy-start = (bf16[1,512,2048]{2,1,0:T(8,128)(2,1)S(1)}, bf16[1,512,2048]{2,1,0:T(8,128)(2,1)}, u32[]{:S(2)}) copy-start(bf16[1,512,2048]{2,1,0:T(8,128)(2,1)} %param.19) | copy-start | bytes 6291460
  6.5 114.8 %copy-start.6 = (f32[1,512]{1,0:T(1,128)S(1)}, f32[1,512]{1,0:T(1,128)}, u32[]{:S(2)}) copy-start(f32[1,512]{1,0:T(1,128)} %param.18) | copy-start | bytes 6148
  6.5 114.8 %all-gather.2.cloned.1.call-start = ((), (), s32[]{:S(2)}) async-start(), calls=%async_computation.4 | async-start | bytes 13369344 | tf_op jit(solution)/shard_map/all_gather | solution.py:91
  30.7 204.6 %reduce-scatter.3.cloned.1.call-start = ((), (), s32[]{:S(2)}) async-start(), calls=%async_computation.5 | async-start | bytes 13369344 | tf_op jit(solution)/shard_map/reduce_scatter | solution.py:98
  140.8 111.9 %copy-start.1 = (bf16[128,2048]{1,0:T(8,128)(2,1)S(1)}, bf16[128,2048]{1,0:T(8,128)(2,1)}, u32[]{:S(2)}) copy-start(bf16[128,2048]{1,0:T(8,128)(2,1)} %param.13) | copy-start | bytes 1572868
  140.8 112.3 %copy-start.2 = (f32[8,2048]{1,0:T(8,128)S(1)}, f32[8,2048]{1,0:T(8,128)}, u32[]{:S(2)}) copy-start(f32[8,2048]{1,0:T(8,128)} %param.20) | copy-start | bytes 196612
  235.3 17.4 %all-to-all-start.1 = ((bf16[8,24,2048]{2,1,0:T(8,128)(2,1)}), bf16[8,24,2048]{2,1,0:T(8,128)(2,1)S(1)}, u32[]{:S(2)}, u32[]{:S(2)}) async-start(bf16[8,24,2048]{2,1,0:T(8,128)(2,1)} %bitcast.23), calls=%async_computation.2 | async-start | bytes 1572864 | tf_op jit(solution)/shard_map/all_to_all | solution.py:104
  239.6 108.3 %reduce-scatter.5.cloned.1.call-start = ((), (), s32[]{:S(2)}) async-start(), calls=%async_computation.6 | async-start | bytes 4718592 | tf_op jit(solution)/shard_map/reduce_scatter | solution.py:125
  253.1 3.9 %copy-start.3 = (f32[2048]{0:T(1024)S(1)}, f32[2048]{0:T(1024)}, u32[]{:S(2)}) copy-start(f32[2048]{0:T(1024)} %param.21) | copy-start | bytes 24580
  258.1 40.7 %copy-start.5 = (f32[1024]{0:T(1024)S(1)}, f32[1024]{0:T(1024)}, u32[]{:S(2)}) copy-start(f32[1024]{0:T(1024)} %param.23) | copy-start | bytes 12292
  258.1 9.9 %collective-permute-start = (bf16[128,2048]{1,0:T(8,128)(2,1)S(1)}, bf16[128,2048]{1,0:T(8,128)(2,1)}, u32[]{:S(2)}, u32[]{:S(2)}) collective-permute-start(bf16[128,2048]{1,0:T(8,128)(2,1)S(1)} %get-tuple-element.6), channel_id=1, source_target_pairs={{0,16},{16,32},{32,48},{48,64},{64,80},{80,96},{96,112},{112,0},{1... | collective-permute-start | bytes 1572872 | tf_op jit(solution)/shard_map/ppermute | solution.py:47
  258.1 9.9 %collective-permute-start.1 = (bf16[128,2048]{1,0:T(8,128)(2,1)S(1)}, bf16[128,2048]{1,0:T(8,128)(2,1)}, u32[]{:S(2)}, u32[]{:S(2)}) collective-permute-start(bf16[128,2048]{1,0:T(8,128)(2,1)S(1)} %get-tuple-element.6), channel_id=1, source_target_pairs={{0,112},{16,0},{32,16},{48,32},{64,48},{80,64},{96,80},{112,96},{1... | collective-permute-start | bytes 1572872 | tf_op jit(solution)/shard_map/ppermute | solution.py:52
  268.0 10.1 %collective-permute-start.2 = (bf16[128,2048]{1,0:T(8,128)(2,1)}, bf16[128,2048]{1,0:T(8,128)(2,1)}, u32[]{:S(2)}, u32[]{:S(2)}) collective-permute-start(bf16[128,2048]{1,0:T(8,128)(2,1)} %collective-permute-done), channel_id=1, source_target_pairs={{0,16},{16,32},{32,48},{48,64},{64,80},{80,96},{96,112},{112,0},{1... | collective-permute-start | bytes 1572872 | tf_op jit(solution)/shard_map/ppermute | solution.py:47
  268.0 13.9 %collective-permute-start.3 = (bf16[128,2048]{1,0:T(8,128)(2,1)}, bf16[128,2048]{1,0:T(8,128)(2,1)}, u32[]{:S(2)}, u32[]{:S(2)}) collective-permute-start(bf16[128,2048]{1,0:T(8,128)(2,1)} %collective-permute-done.1), channel_id=1, source_target_pairs={{0,112},{16,0},{32,16},{48,32},{64,48},{80,64},{96,80},{112,96},{1... | collective-permute-start | bytes 1572872 | tf_op jit(solution)/shard_map/ppermute | solution.py:52
  278.1 10.0 %collective-permute-start.4 = (bf16[128,2048]{1,0:T(8,128)(2,1)}, bf16[128,2048]{1,0:T(8,128)(2,1)S(1)}, u32[]{:S(2)}, u32[]{:S(2)}) collective-permute-start(bf16[128,2048]{1,0:T(8,128)(2,1)} %collective-permute-done.2), channel_id=1, source_target_pairs={{0,16},{16,32},{32,48},{48,64},{64,80},{80,96},{96,112},{112,0},{1... | collective-permute-start | bytes 1572872 | tf_op jit(solution)/shard_map/ppermute | solution.py:47
  281.9 9.9 %collective-permute-start.5 = (bf16[128,2048]{1,0:T(8,128)(2,1)}, bf16[128,2048]{1,0:T(8,128)(2,1)S(1)}, u32[]{:S(2)}, u32[]{:S(2)}) collective-permute-start(bf16[128,2048]{1,0:T(8,128)(2,1)} %collective-permute-done.3), channel_id=1, source_target_pairs={{0,112},{16,0},{32,16},{48,32},{64,48},{80,64},{96,80},{112,96},{1... | collective-permute-start | bytes 1572872 | tf_op jit(solution)/shard_map/ppermute | solution.py:52
  288.2 9.8 %collective-permute-start.6 = (bf16[128,2048]{1,0:T(8,128)(2,1)S(1)}, bf16[128,2048]{1,0:T(8,128)(2,1)S(1)}, u32[]{:S(2)}, u32[]{:S(2)}) collective-permute-start(bf16[128,2048]{1,0:T(8,128)(2,1)S(1)} %collective-permute-done.4), channel_id=1, source_target_pairs={{0,16},{16,32},{32,48},{48,64},{64,80},{80,96},{96,112},{112,0},{1... | collective-permute-start | bytes 1572872 | tf_op jit(solution)/shard_map/ppermute | solution.py:47
  313.2 34.7 %copy-start.4 = (f32[2048]{0:T(1024)S(1)}, f32[2048]{0:T(1024)}, u32[]{:S(2)}) copy-start(f32[2048]{0:T(1024)} %param.25) | copy-start | bytes 24580
Sparse Core Ops, SparseCore 0:
  30.8 90.4 all-gather.1
  141.0 94.2 reduce-scatter.2
  313.3 34.5 reduce-scatter.4
